TPU v7x, 32 devices: a whole 2x2x4 slice. The times are simulated.
32 devices in a mesh: row: 8 (over y, x, core), col: 4 (over z).
Axes of the slice: x: 2, y: 2, z: 4, core: 2. Of those that a mesh axis runs over, the one named last changes fastest.
Arguments:
- inverse: float32 [4096, 4096], P('row', 'col'), may hold values from -0.05 to 0.05
- owner: int32 [32], replicated, may hold values from 0 to 31, each once
- struct_parent: int32 [32], replicated, may hold values 0 or 1
- struct_child: int32 [32], replicated, may hold values 0 or 1
- panel_parent: float32 [4096, 1024], P('row', 'col'), may hold values from -1.5 to 1.5
- panel_child: float32 [4096, 1024], P('row', 'col'), may hold values from -1.5 to 1.5
- child_on_parent: float32 [1024, 1024], P('col'), may hold values from -0.1875 to 0.1875
- dinv_parent: float32 [1024, 1024], P('col'), may hold values from -6 to 6
- dinv_child: float32 [1024, 1024], P('col'), may hold values from -6 to 6
Outputs:
- row_parent: float32 [1024, 4096], P('col', 'row')
- inv_parent: float32 [1024, 1024], P('col')
- row_child: float32 [1024, 4096], P('col', 'row')
- inv_cross: float32 [1024, 1024], P('col')
- inv_child: float32 [1024, 1024], P('col')
Inputs may be any that keep to these rules, and one draw needn't show every extreme that they name: `owner`: each slot holds a different block.
All inputs are finite; a program needn't handle non-finite values.
Results may differ from a plain program's by a relative error of at most 0.000071.
Values sent between devices are 32-bit elements; how exact they have to be, the bound alone decides.
A program may use at most 128 MiB of HBM per device.

v0:
```python
import jax
import jax.numpy as jnp
from jax import lax
from jax.sharding import PartitionSpec as P

BLOCK_ROWS = 128
HIGHEST = lax.Precision.HIGHEST


def broadcast(block, axis, source):
    block = jnp.where(lax.axis_index(axis) == source, block, jnp.zeros_like(block))
    return lax.psum(block, axis)


def contract_first(left, right):
    return lax.dot_general(
        left, right, (((0,), (0,)), ((), ())), precision=HIGHEST, preferred_element_type=jnp.float32
    )


def contract_cross(left, right):
    return lax.dot_general(
        left, right, (((0,), (1,)), ((), ())), precision=HIGHEST, preferred_element_type=jnp.float32
    )


def matmul(left, right):
    return jnp.dot(left, right, precision=HIGHEST, preferred_element_type=jnp.float32)


def per_device(
    inverse,
    owner,
    struct_parent,
    struct_child,
    panel_parent,
    panel_child,
    child_on_parent,
    dinv_parent,
    dinv_child,
):
    rows_dev = inverse.shape[0]
    nblocks = owner.shape[0]
    ratio = lax.axis_size("row") // lax.axis_size("col")
    row_at = lax.axis_index("row")
    col_at = lax.axis_index("col")
    row_tiles = rows_dev // BLOCK_ROWS
    matches = owner[:, None] == jnp.arange(nblocks, dtype=jnp.int32)[None, :]
    live_parent = jnp.sum(jnp.where(matches, struct_parent[None, :], 0), axis=1)
    live_child = live_parent * jnp.sum(jnp.where(matches, struct_child[None, :], 0), axis=1)
    parent_rowblk = lax.dynamic_slice_in_dim(live_parent, row_at * row_tiles, row_tiles)
    child_rowblk = lax.dynamic_slice_in_dim(live_child, row_at * row_tiles, row_tiles)
    mask_parent = jnp.repeat(parent_rowblk.astype(jnp.float32), BLOCK_ROWS)
    mask_child = jnp.repeat(child_rowblk.astype(jnp.float32), BLOCK_ROWS)
    masked_parent = panel_parent * mask_parent[:, None]
    masked_child = panel_child * mask_child[:, None]
    full_parent, full_child = (
        lax.all_gather(masked_parent, "col", axis=1, tiled=True),
        lax.all_gather(masked_child, "col", axis=1, tiled=True),
    )
    parent_pieces = []
    child_pieces = []
    for offset in range(ratio):
        got_parent, got_child = (
            broadcast(full_parent, "row", ratio * col_at + offset),
            broadcast(full_child, "row", ratio * col_at + offset),
        )
        parent_pieces.append(got_parent)
        child_pieces.append(got_child)
    column_parent = jnp.concatenate(parent_pieces, axis=0)
    column_child = jnp.concatenate(child_pieces, axis=0)

    def region_term(panel):
        return contract_cross(panel, inverse)

    row_parent = (
        -lax.psum_scatter(region_term(column_parent), "col", scatter_dimension=0, tiled=True)
        * mask_parent[None, :]
    )
    sum_parent, sum_cross = lax.psum(
        (matmul(row_parent, full_parent), matmul(row_parent, full_child)), "row"
    )
    inv_parent = dinv_parent - sum_parent
    parent_full = lax.all_gather(child_on_parent, "col", axis=0, tiled=True)
    inv_cross = -(sum_cross + matmul(inv_parent, parent_full))
    row_child = (
        -lax.psum_scatter(
            region_term(column_child) + contract_first(child_on_parent, row_parent),
            "col",
            scatter_dimension=0,
            tiled=True,
        )
        * mask_child[None, :]
    )
    sum_child = lax.psum(matmul(row_child, full_child), "row")
    cross_term = lax.psum_scatter(
        contract_first(inv_cross, child_on_parent), "col", scatter_dimension=0, tiled=True
    )
    inv_child = dinv_child - sum_child - cross_term
    return (row_parent, inv_parent, row_child, inv_cross, inv_child)


def solution(mesh):
    return jax.shard_map(
        per_device,
        mesh=mesh,
        in_specs=(
            P("row", "col"),
            P(),
            P(),
            P(),
            P("row", "col"),
            P("row", "col"),
            P("col", None),
            P("col", None),
            P("col", None),
        ),
        out_specs=(
            P("col", "row"),
            P("col", None),
            P("col", "row"),
            P("col", None),
            P("col", None),
        ),
        check_vma=False,
    )
```

profile of v0, /device:TPU:0, one launch (start us, length us, event | category | flops | bytes accessed | tf_op | source)
XLA Modules:
  0.0 599.8 jit_solution(15787337251794330934)
XLA Ops:
  7.2 1.0 select_reduce_fusion
  8.4 2.0 broadcast_multiply_fusion
  10.6 2.0 broadcast_multiply_fusion.1
  12.7 46.3 %all-gather.6.cloned.1.call-done = f32[512,1024]{1,0:T(8,128)} async-done(((f32[512,256]{1,0:T(8,128)}), f32[512,1024]{1,0:T(8,128)}) %all-gather.6.cloned.1.call-update) | async-done | bytes 2097168 | tf_op jit(solution)/shard_map/all_gather | solution.py:59
  58.9 4.2 broadcast_select_fusion.1
  63.2 42.4 %all-gather.4.cloned.1.call-done = f32[512,1024]{1,0:T(8,128)} async-done(((f32[512,256]{1,0:T(8,128)}), f32[512,1024]{1,0:T(8,128)}) %all-gather.4.cloned.1.call-update) | async-done | bytes 2097168 | tf_op jit(solution)/shard_map/all_gather | solution.py:58
  105.6 4.2 broadcast_select_fusion.3
  109.9 125.1 %all-reduce.7.cloned.1.call-done = (f32[512,1024]{1,0:T(8,128)}, f32[512,1024]{1,0:T(8,128)}, f32[512,1024]{1,0:T(8,128)}, f32[512,1024]{1,0:T(8,128)}) async-done(((f32[512,1024]{1,0:T(8,128)}, f32[512,1024]{1,0:T(8,128)}, f32[512,1024]{1,0:T(8,128)}, f32[512,1024]{1,0:T(8,128)}), (f32[512,1024]{1,0:T(8,128)}, f32[512,1024]{1,0:T(8,128)}, f32[512,1024]{1,0:T(8,128)}, ...) | async-done | bytes 8388624 | tf_op jit(solution)/shard_map/psum | solution.py:12
  235.0 16.0 %fusion = f32[1024,512]{1,0:T(8,128)} fusion(f32[512,1024]{1,0:T(8,128)S(1)} %copy-done, f32[512,1024]{1,0:T(8,128)} %get-tuple-element.10, f32[512,1024]{1,0:T(8,128)} %get-tuple-element.11), kind=kOutput, calls=%fused_computation | convolution fusion | flops 6443499520 | bytes 8388608 | tf_op jit(solution)/shard_map/dot_general | solution.py:22
  251.0 0.2 reduce-scatter.6.cloned.1.call-start
  251.2 16.1 %fusion.4 = f32[1024,512]{1,0:T(8,128)} fusion(f32[512,1024]{1,0:T(8,128)S(1)} %copy-done, f32[512,1024]{1,0:T(8,128)} %get-tuple-element.12, f32[512,1024]{1,0:T(8,128)} %get-tuple-element.13), kind=kOutput, calls=%fused_computation.4 | convolution fusion | flops 6443499520 | bytes 8388608 | tf_op jit(solution)/shard_map/dot_general | solution.py:22
  267.3 27.6 %reduce-scatter.4.cloned.1.call-done = f32[256,512]{1,0:T(8,128)} async-done(((f32[1024,512]{1,0:T(8,128)}), f32[256,512]{1,0:T(8,128)}) %reduce-scatter.4.cloned.1.call-update) | async-done | bytes 524304 | tf_op jit(solution)/shard_map/reduce_scatter | solution.py:77
  294.9 1.1 negate_multiply_fusion.1
  296.0 0.8 copy-done.4
  296.8 4.9 bitcast_add_fusion
  301.7 0.3 all-reduce.5.cloned.1.call-start
  302.0 0.7 copy-done.5
  302.7 4.6 fusion.12
  307.3 2.9 fusion.11
  310.2 34.5 %reduce-scatter.6.cloned.1.call-done = f32[256,512]{1,0:T(8,128)} async-done(((f32[1024,512]{1,0:T(8,128)}), f32[256,512]{1,0:T(8,128)}) %reduce-scatter.6.cloned.1.call-update) | async-done | bytes 524304 | tf_op jit(solution)/shard_map/reduce_scatter | solution.py:87
  344.7 1.1 negate_multiply_fusion
  345.8 0.8 copy-done.8
  346.6 4.5 fusion.13
  351.1 0.7 all-gather.8.cloned.1.call-update
  351.9 68.0 %all-reduce.5.cloned.1.call-done = (f32[256,1024]{1,0:T(8,128)}, f32[256,1024]{1,0:T(8,128)}, f32[256,1024]{1,0:T(8,128)}) async-done(((f32[256,1024]{1,0:T(8,128)}, f32[256,1024]{1,0:T(8,128)}, f32[256,1024]{1,0:T(8,128)}), (f32[256,1024]{1,0:T(8,128)}, f32[256,1024]{1,0:T(8,128)}, f32[256,1024]{1,0:T(8,128)})) %all-reduce.5.cloned.1.call-update) | async-done | bytes 3145744 | tf_op jit(solution)/shard_map/psum | solution.py:80
  419.9 1.7 sub.9
  421.5 80.7 %all-gather.8.cloned.1.call-done = f32[1024,1024]{1,0:T(8,128)} async-done(((f32[256,1024]{1,0:T(8,128)}), f32[1024,1024]{1,0:T(8,128)}) %all-gather.8.cloned.1.call-update) | async-done | bytes 4194320 | tf_op jit(solution)/shard_map/all_gather | solution.py:84
  502.3 6.3 %fusion.8 = f32[256,1024]{1,0:T(8,128)S(1)} fusion(f32[256,1024]{1,0:T(8,128)} %get-tuple-element.8, f32[256,1024]{1,0:T(8,128)S(1)} %sub.9, f32[1024,1024]{1,0:T(8,128)} %all-gather.8.cloned.1.call-done), kind=kOutput, calls=%fused_computation.10 | convolution fusion | flops 3221749760 | bytes 7340032 | tf_op jit(solution)/shard_map/dot_general | solution.py:28
  508.6 1.0 copy-done.7
  509.6 5.1 fusion.14
  514.7 75.4 %reduce-scatter.8.cloned.1.call-done = f32[256,1024]{1,0:T(8,128)} async-done(((f32[1024,1024]{1,0:T(8,128)}), f32[256,1024]{1,0:T(8,128)}) %reduce-scatter.8.cloned.1.call-update) | async-done | bytes 1048592 | tf_op jit(solution)/shard_map/reduce_scatter | solution.py:96
  590.1 2.8 subtract_subtract_fusion
  (34 shorter events, 0.7 us)
Async XLA Ops:
  7.2 227.8 %copy-start = (f32[512,1024]{1,0:T(8,128)S(1)}, f32[512,1024]{1,0:T(8,128)}, u32[]{:S(2)}) copy-start(f32[512,1024]{1,0:T(8,128)} %param.9) | copy-start | bytes 6291460
  7.2 51.8 %all-gather.6.cloned.1.call-start = ((), (), s32[]{:S(2)}) async-start(), calls=%async_computation.5 | async-start | bytes 2621440 | tf_op jit(solution)/shard_map/all_gather | solution.py:59
  10.4 95.2 %all-gather.4.cloned.1.call-start = ((), (), s32[]{:S(2)}) async-start(), calls=%async_computation.3 | async-start | bytes 2621440 | tf_op jit(solution)/shard_map/all_gather | solution.py:58
  12.6 222.4 %all-reduce.7.cloned.1.call-start = ((), (), s32[]{:S(2)}) async-start(), calls=%async_computation.10 | async-start | bytes 16777216 | tf_op jit(solution)/shard_map/psum | solution.py:12
  109.8 185.1 %reduce-scatter.4.cloned.1.call-start = ((), (), s32[]{:S(2)}) async-start(), calls=%async_computation.4 | async-start | bytes 2621440 | tf_op jit(solution)/shard_map/reduce_scatter | solution.py:77
  251.0 93.7 %reduce-scatter.6.cloned.1.call-start = ((), (), s32[]{:S(2)}) async-start(), calls=%async_computation.6 | async-start | bytes 2621440 | tf_op jit(solution)/shard_map/reduce_scatter | solution.py:87
  251.2 45.6 %copy-start.1 = (f32[256,1024]{1,0:T(8,128)S(1)}, f32[256,1024]{1,0:T(8,128)}, u32[]{:S(2)}) copy-start(f32[256,1024]{1,0:T(8,128)} %param.15) | copy-start | bytes 3145732
  296.0 0.8 copy-start.4
  301.7 1.0 copy-start.5
  301.7 118.1 %all-reduce.5.cloned.1.call-start = ((), (), s32[]{:S(2)}) async-start(), calls=%async_computation.9 | async-start | bytes 6291456 | tf_op jit(solution)/shard_map/psum | solution.py:80
  302.7 4.6 copy-start.3
  345.8 0.8 copy-start.8
  351.1 151.2 %all-gather.8.cloned.1.call-start = ((), (), s32[]{:S(2)}) async-start(), calls=%async_computation.7 | async-start | bytes 5242880 | tf_op jit(solution)/shard_map/all_gather | solution.py:84
  351.8 238.3 %reduce-scatter.8.cloned.1.call-start = ((), (), s32[]{:S(2)}) async-start(), calls=%async_computation.8 | async-start | bytes 5242880 | tf_op jit(solution)/shard_map/reduce_scatter | solution.py:96
  421.5 87.1 %copy-start.6 = (f32[256,1024]{1,0:T(8,128)}, f32[256,1024]{1,0:T(8,128)S(1)}, u32[]{:S(2)}) copy-start(f32[256,1024]{1,0:T(8,128)S(1)} %sub.9) | copy-start | bytes 3145732
  502.3 7.3 %copy-start.2 = (f32[256,1024]{1,0:T(8,128)S(1)}, f32[256,1024]{1,0:T(8,128)}, u32[]{:S(2)}) copy-start(f32[256,1024]{1,0:T(8,128)} %param.15) | copy-start | bytes 3145732
  508.6 1.0 copy-start.7
  514.7 75.5 %copy-start.9 = (f32[256,1024]{1,0:T(8,128)S(1)}, f32[256,1024]{1,0:T(8,128)}, u32[]{:S(2)}) copy-start(f32[256,1024]{1,0:T(8,128)} %param.17) | copy-start | bytes 3145732
Sparse Core Ops, SparseCore 0:
  10.5 48.3 all-gather.5
  61.1 44.4 all-gather.3
  109.9 125.0 all-reduce.6
  251.1 43.7 reduce-scatter.3
  301.8 42.8 reduce-scatter.5
  351.2 68.6 all-reduce.4
  421.4 80.8 all-gather.7
  514.8 75.2 reduce-scatter.7
where the time goes:
time: 600 us
  waiting for transfers between devices  501 us (84%)
  matrix products  60.2 us (10%)
  other arithmetic  20.2 us (3%)
  between operations  14.3 us (2%)
    psum x1, waiting for transfers between devices, broadcast(): return lax.psum(block, axis)  125 us
    all_gather x1, waiting for transfers between devices, per_device(): parent_full = lax.all_gather(child_on_parent, 'col', axis=0, tiled=True)  80.7 us
    reduce_scatter x1, waiting for transfers between devices, per_device(): lax.psum_scatter(contract_first(inv_cross, child_on_parent), 'col', scatt...  75.4 us
    psum x1, waiting for transfers between devices, per_device(): lax.psum((matmul(row_parent, full_parent), matmul(row_parent, full_child)...  68 us
    all_gather x1, waiting for transfers between devices, per_device(): lax.all_gather(masked_child, 'col', axis=1, tiled=True)  46.3 us
    all_gather x1, waiting for transfers between devices, per_device(): lax.all_gather(masked_parent, 'col', axis=1, tiled=True)  42.4 us
    reduce_scatter x1, waiting for transfers between devices, per_device(): lax.psum_scatter(region_term(column_child) + contract_first(child_on_pare...  34.5 us
    dot_general x2, matrix products, contract_cross(): lax.dot_general(left, right, (((0,), (1,)), ((), ())), precision=HIGHEST,...  32 us
  transfers between devices with their start and end apart: 8, of which 8 were waited for; matrix products, arithmetic and copies ran while one was open for 5% of the time, Pallas kernels for 0%

commit v1 on v0

--- a/solution.py
+++ b/solution.py
@@ -2,6 +2,7 @@
 import jax.numpy as jnp
 from jax import lax
 from jax.sharding import PartitionSpec as P
+from jax.lax import all_gather
 
 BLOCK_ROWS = 128
 HIGHEST = lax.Precision.HIGHEST
@@ -9,7 +10,7 @@
 
 def broadcast(block, axis, source):
     block = jnp.where(lax.axis_index(axis) == source, block, jnp.zeros_like(block))
-    return lax.psum(block, axis)
+    return jnp.sum(all_gather(block, axis), 0)
 
 
 def contract_first(left, right):

time: 600 us -> 831 us (1.39); the launches traced: 600 us -> 821 us
  waiting for transfers between devices: 501 us -> 675 us
  other arithmetic: 20.2 us -> 57.6 us
  starting transfers between devices: 0.73 us -> 9.99 us
    all_gather x0 -> x4, waiting for transfers between devices: none -> 306 us  [broadcast(): return jnp.sum(all_gather(block, axis), 0)]
    psum x1 -> x0, waiting for transfers between devices: 125 us -> none  [broadcast(): return lax.psum(block, axis)]
    reduce_sum x0 -> x4, other arithmetic: none -> 37.3 us  [broadcast(): return jnp.sum(all_gather(block, axis), 0)]
    reduce_scatter x1, starting transfers between devices: 0.22 us -> 9.4 us  [per_device(): lax.psum_scatter(region_term(column_child) + contract_first(child_on_pare...]
  transfers between devices with their start and end apart: 8 -> 11, of which waited for: 8 -> 11; matrix products, arithmetic and copies ran while one was open for 5% -> 11% of each run, Pallas kernels for 0% -> 0%
where the time goes in v1:
time: 831 us; the launch traced here: 821 us
  waiting for transfers between devices  675 us (81%)
  matrix products  60.4 us (7%)
  other arithmetic  57.6 us (7%)
  between operations  14.4 us (2%)
  starting transfers between devices  9.99 us (1%)
    all_gather x4, waiting for transfers between devices, broadcast(): return jnp.sum(all_gather(block, axis), 0)  306 us
    all_gather x1, waiting for transfers between devices, per_device(): parent_full = lax.all_gather(child_on_parent, 'col', axis=0, tiled=True)  80.6 us
    reduce_scatter x1, waiting for transfers between devices, per_device(): lax.psum_scatter(contract_first(inv_cross, child_on_parent), 'col', scatt...  75.4 us
    psum x1, waiting for transfers between devices, per_device(): lax.psum((matmul(row_parent, full_parent), matmul(row_parent, full_child)...  68.2 us
    all_gather x1, waiting for transfers between devices, per_device(): lax.all_gather(masked_parent, 'col', axis=1, tiled=True)  46.3 us
    all_gather x1, waiting for transfers between devices, per_device(): lax.all_gather(masked_child, 'col', axis=1, tiled=True)  41.7 us
    reduce_sum x4, other arithmetic, broadcast(): return jnp.sum(all_gather(block, axis), 0)  37.3 us
    reduce_scatter x1, waiting for transfers between devices, per_device(): lax.psum_scatter(region_term(column_child) + contract_first(child_on_pare...  34.5 us
  transfers between devices with their start and end apart: 11, of which 11 were waited for; matrix products, arithmetic and copies ran while one was open for 11% of the time, Pallas kernels for 0%

profile of v1, /device:TPU:0, one launch (start us, length us, event | category | flops | bytes accessed | tf_op | source)
XLA Modules:
  0.0 821.2 jit_solution(7396953306050971827)
XLA Ops:
  8.4 2.0 broadcast_multiply_fusion.1
  10.6 2.0 broadcast_multiply_fusion
  12.7 46.3 %all-gather.12.cloned.1.call-done = f32[512,1024]{1,0:T(8,128)} async-done(((f32[512,256]{1,0:T(8,128)}), f32[512,1024]{1,0:T(8,128)}) %all-gather.12.cloned.1.call-update) | async-done | bytes 2097168 | tf_op jit(solution)/shard_map/all_gather | solution.py:59
  58.9 4.3 broadcast_select_fusion.3
  63.9 41.7 %all-gather.14.cloned.1.call-done = f32[512,1024]{1,0:T(8,128)} async-done(((f32[512,256]{1,0:T(8,128)}), f32[512,1024]{1,0:T(8,128)}) %all-gather.14.cloned.1.call-update) | async-done | bytes 2097168 | tf_op jit(solution)/shard_map/all_gather | solution.py:60
  105.6 4.3 broadcast_select_fusion.1
  110.5 85.5 %all-gather.18.cloned.1.call-done = f32[4096,1024]{1,0:T(8,128)} async-done(((f32[512,1024]{1,0:T(8,128)}), f32[4096,1024]{1,0:T(8,128)}) %all-gather.18.cloned.1.call-update) | async-done | bytes 16777232 | tf_op jit(solution)/shard_map/all_gather | solution.py:13
  196.0 9.3 %reduce_sum.55 = f32[512,1024]{1,0:T(8,128)} reduce(f32[8,512,1024]{2,1,0:T(8,128)} %bitcast.24, f32[]{:T(128)} %constant.20.clone.1), dimensions={0}, to_apply=%region_1.2 | reduce | flops 3670016 | bytes 18874372 | tf_op jit(solution)/shard_map/reduce_sum | solution.py:13
  205.3 82.2 %all-gather.20.cloned.1.call-done = f32[4096,1024]{1,0:T(8,128)} async-done(((f32[512,1024]{1,0:T(8,128)}), f32[4096,1024]{1,0:T(8,128)}) %all-gather.20.cloned.1.call-update) | async-done | bytes 16777232 | tf_op jit(solution)/shard_map/all_gather | solution.py:13
  287.5 9.3 %reduce_sum.56 = f32[512,1024]{1,0:T(8,128)} reduce(f32[8,512,1024]{2,1,0:T(8,128)} %bitcast.25, f32[]{:T(128)} %constant.20.clone.1), dimensions={0}, to_apply=%region_2.3 | reduce | flops 3670016 | bytes 18874372 | tf_op jit(solution)/shard_map/reduce_sum | solution.py:13
  296.8 16.3 %fusion = f32[1024,512]{1,0:T(8,128)} fusion(f32[512,1024]{1,0:T(8,128)S(1)} %copy-done, f32[512,1024]{1,0:T(8,128)} %reduce_sum.56, f32[512,1024]{1,0:T(8,128)} %reduce_sum.55), kind=kOutput, calls=%fused_computation | convolution fusion | flops 6443499520 | bytes 8388608 | tf_op jit(solution)/shard_map/dot_general | solution.py:23
  313.2 9.4 %reduce-scatter.6.cloned.1.call-start = ((), (), s32[]{:S(2)}) async-start(), calls=%async_computation.6 | async-start | bytes 2621440 | tf_op jit(solution)/shard_map/reduce_scatter | solution.py:88
  322.6 56.4 %all-gather.22.cloned.1.call-done = f32[4096,1024]{1,0:T(8,128)} async-done(((f32[512,1024]{1,0:T(8,128)}), f32[4096,1024]{1,0:T(8,128)}) %all-gather.22.cloned.1.call-update) | async-done | bytes 16777232 | tf_op jit(solution)/shard_map/all_gather | solution.py:13
  379.0 9.4 %reduce_sum.58 = f32[512,1024]{1,0:T(8,128)} reduce(f32[8,512,1024]{2,1,0:T(8,128)} %bitcast.26, f32[]{:T(128)} %constant.20.clone.1), dimensions={0}, to_apply=%region_6.7 | reduce | flops 3670016 | bytes 18874372 | tf_op jit(solution)/shard_map/reduce_sum | solution.py:13
  388.4 82.1 %all-gather.24.cloned.1.call-done = f32[4096,1024]{1,0:T(8,128)} async-done(((f32[512,1024]{1,0:T(8,128)}), f32[4096,1024]{1,0:T(8,128)}) %all-gather.24.cloned.1.call-update) | async-done | bytes 16777232 | tf_op jit(solution)/shard_map/all_gather | solution.py:13
  470.5 9.3 %reduce_sum.59 = f32[512,1024]{1,0:T(8,128)} reduce(f32[8,512,1024]{2,1,0:T(8,128)} %bitcast.27, f32[]{:T(128)} %constant.20.clone.1), dimensions={0}, to_apply=%region_7.8 | reduce | flops 3670016 | bytes 18874372 | tf_op jit(solution)/shard_map/reduce_sum | solution.py:13
  479.8 16.0 %fusion.4 = f32[1024,512]{1,0:T(8,128)} fusion(f32[512,1024]{1,0:T(8,128)S(1)} %copy-done, f32[512,1024]{1,0:T(8,128)} %reduce_sum.59, f32[512,1024]{1,0:T(8,128)} %reduce_sum.58), kind=kOutput, calls=%fused_computation.4 | convolution fusion | flops 6443499520 | bytes 8388608 | tf_op jit(solution)/shard_map/dot_general | solution.py:23
  495.8 20.6 %reduce-scatter.4.cloned.1.call-done = f32[256,512]{1,0:T(8,128)} async-done(((f32[1024,512]{1,0:T(8,128)}), f32[256,512]{1,0:T(8,128)}) %reduce-scatter.4.cloned.1.call-update) | async-done | bytes 524304 | tf_op jit(solution)/shard_map/reduce_scatter | solution.py:78
  516.5 1.1 negate_multiply_fusion.1
  518.4 4.8 bitcast_add_fusion
  524.2 4.6 fusion.12
  528.8 2.9 fusion.11
  531.7 34.5 %reduce-scatter.6.cloned.1.call-done = f32[256,512]{1,0:T(8,128)} async-done(((f32[1024,512]{1,0:T(8,128)}), f32[256,512]{1,0:T(8,128)}) %reduce-scatter.6.cloned.1.call-update) | async-done | bytes 524304 | tf_op jit(solution)/shard_map/reduce_scatter | solution.py:88
  566.2 1.1 negate_multiply_fusion
  568.1 4.5 fusion.13
  573.2 68.2 %all-reduce.3.cloned.1.call-done = (f32[256,1024]{1,0:T(8,128)}, f32[256,1024]{1,0:T(8,128)}, f32[256,1024]{1,0:T(8,128)}) async-done(((f32[256,1024]{1,0:T(8,128)}, f32[256,1024]{1,0:T(8,128)}, f32[256,1024]{1,0:T(8,128)}), (f32[256,1024]{1,0:T(8,128)}, f32[256,1024]{1,0:T(8,128)}, f32[256,1024]{1,0:T(8,128)})) %all-reduce.3.cloned.1.call-update) | async-done | bytes 3145744 | tf_op jit(solution)/shard_map/psum | solution.py:81
  641.4 1.7 sub.9
  643.1 80.6 %all-gather.16.cloned.1.call-done = f32[1024,1024]{1,0:T(8,128)} async-done(((f32[256,1024]{1,0:T(8,128)}), f32[1024,1024]{1,0:T(8,128)}) %all-gather.16.cloned.1.call-update) | async-done | bytes 4194320 | tf_op jit(solution)/shard_map/all_gather | solution.py:85
  723.6 6.3 fusion.8
  731.0 5.1 fusion.14
  736.1 75.4 %reduce-scatter.8.cloned.1.call-done = f32[256,1024]{1,0:T(8,128)} async-done(((f32[1024,1024]{1,0:T(8,128)}), f32[256,1024]{1,0:T(8,128)}) %reduce-scatter.8.cloned.1.call-update) | async-done | bytes 1048592 | tf_op jit(solution)/shard_map/reduce_scatter | solution.py:97
  811.5 2.8 subtract_subtract_fusion
  (47 shorter events, 7.0 us)
Async XLA Ops:
  7.2 289.7 %copy-start = (f32[512,1024]{1,0:T(8,128)S(1)}, f32[512,1024]{1,0:T(8,128)}, u32[]{:S(2)}) copy-start(f32[512,1024]{1,0:T(8,128)} %param.9) | copy-start | bytes 6291460
  7.2 51.7 %all-gather.12.cloned.1.call-start = ((), (), s32[]{:S(2)}) async-start(), calls=%async_computation.3 | async-start | bytes 2621440 | tf_op jit(solution)/shard_map/all_gather | solution.py:59
  10.4 95.2 %all-gather.14.cloned.1.call-start = ((), (), s32[]{:S(2)}) async-start(), calls=%async_computation.5 | async-start | bytes 2621440 | tf_op jit(solution)/shard_map/all_gather | solution.py:60
  12.6 183.4 %all-gather.18.cloned.1.call-start = ((), (), s32[]{:S(2)}) async-start(), calls=%async_computation.9 | async-start | bytes 18874368 | tf_op jit(solution)/shard_map/all_gather | solution.py:13
  63.2 224.3 %all-gather.20.cloned.1.call-start = ((), (), s32[]{:S(2)}) async-start(), calls=%async_computation.10 | async-start | bytes 18874368 | tf_op jit(solution)/shard_map/all_gather | solution.py:13
  63.8 315.2 %all-gather.22.cloned.1.call-start = ((), (), s32[]{:S(2)}) async-start(), calls=%async_computation.11 | async-start | bytes 18874368 | tf_op jit(solution)/shard_map/all_gather | solution.py:13
  109.9 360.6 %all-gather.24.cloned.1.call-start = ((), (), s32[]{:S(2)}) async-start(), calls=%async_computation.12 | async-start | bytes 18874368 | tf_op jit(solution)/shard_map/all_gather | solution.py:13
  110.5 406.0 %reduce-scatter.4.cloned.1.call-start = ((), (), s32[]{:S(2)}) async-start(), calls=%async_computation.4 | async-start | bytes 2621440 | tf_op jit(solution)/shard_map/reduce_scatter | solution.py:78
  313.2 253.0 %reduce-scatter.6.cloned.1.call-start = ((), (), s32[]{:S(2)}) async-start(), calls=%async_computation.6 | async-start | bytes 2621440 | tf_op jit(solution)/shard_map/reduce_scatter | solution.py:88
  479.8 38.6 %copy-start.1 = (f32[256,1024]{1,0:T(8,128)S(1)}, f32[256,1024]{1,0:T(8,128)}, u32[]{:S(2)}) copy-start(f32[256,1024]{1,0:T(8,128)} %param.15) | copy-start | bytes 3145732
  517.6 0.8 copy-start.4
  523.2 1.0 copy-start.5
  523.2 118.2 %all-reduce.3.cloned.1.call-start = ((), (), s32[]{:S(2)}) async-start(), calls=%async_computation.13 | async-start | bytes 6291456 | tf_op jit(solution)/shard_map/psum | solution.py:81
  524.2 4.6 copy-start.3
  567.3 0.8 copy-start.8
  572.5 151.1 %all-gather.16.cloned.1.call-start = ((), (), s32[]{:S(2)}) async-start(), calls=%async_computation.7 | async-start | bytes 5242880 | tf_op jit(solution)/shard_map/all_gather | solution.py:85
  573.1 238.4 %reduce-scatter.8.cloned.1.call-start = ((), (), s32[]{:S(2)}) async-start(), calls=%async_computation.8 | async-start | bytes 5242880 | tf_op jit(solution)/shard_map/reduce_scatter | solution.py:97
  643.1 86.9 %copy-start.6 = (f32[256,1024]{1,0:T(8,128)}, f32[256,1024]{1,0:T(8,128)S(1)}, u32[]{:S(2)}) copy-start(f32[256,1024]{1,0:T(8,128)S(1)} %sub.9) | copy-start | bytes 3145732
  723.6 7.3 copy-start.2
  730.0 1.0 copy-start.7
  736.0 75.5 %copy-start.9 = (f32[256,1024]{1,0:T(8,128)S(1)}, f32[256,1024]{1,0:T(8,128)}, u32[]{:S(2)}) copy-start(f32[256,1024]{1,0:T(8,128)} %param.17) | copy-start | bytes 3145732
Sparse Core Ops, SparseCore 0:
  10.5 48.3 all-gather.11
  61.1 44.4 all-gather.13
  107.5 88.5 all-gather.17
  197.8 89.7 all-gather.19
  289.3 89.7 all-gather.21
  380.8 89.7 all-gather.23
  472.8 43.6 reduce-scatter.3
  523.3 42.8 reduce-scatter.5
  572.7 68.6 all-reduce.2
  642.8 80.8 all-gather.15
  736.2 75.2 reduce-scatter.7
